TPU v7x, 32 devices: a whole 2x2x4 slice. The times are simulated.
32 devices in a mesh: dp: 8 (over y, x, core), ffn: 4 (over z).
Axes of the slice: x: 2, y: 2, z: 4, core: 2. Of those that a mesh axis runs over, the one named last changes fastest.
Arguments:
- seg_input: bfloat16 [2, 8, 512, 1024], P(None, 'dp', 'ffn'), may hold values from -6 to 6
- memory: bfloat16 [2, 8, 384, 1024], P(None, 'dp', 'ffn'), may hold values from -6 to 6
- compressed: bfloat16 [2, 8, 512, 1024], P(None, 'dp', 'ffn'), may hold values from -6 to 6
- mem_fill: int32 [2, 8], P(None, 'dp'), may hold values from 0 to 384, as said below
- comp_fill: int32 [2, 8], P(None, 'dp'), may hold values from 0 to 512, as said below
- attn_gain: float32 [1024], replicated, may hold values from 0.5 to 1.5
- attn_shift: float32 [1024], replicated, may hold values from -1.75 to 1.75
- attn_weights: bfloat16 [4096, 1024], replicated, may hold values from -1.5 to 1.5
- rel_table: float32 [8, 22], replicated, may hold values from -6 to 6
- ffn_gain: float32 [1024], replicated, may hold values from 0.5 to 1.5
- ffn_shift: float32 [1024], replicated, may hold values from -1.75 to 1.75
- w_up: bfloat16 [1024, 4096], P(None, 'ffn'), may hold values from -0.1875 to 0.1875
- b_up: float32 [4096], P('ffn'), may hold values from -1.75 to 1.75
- w_down: bfloat16 [4096, 1024], P('ffn'), may hold values from -0.125 to 0.125
- b_down: float32 [1024], replicated, may hold values from -1.75 to 1.75
- conv_weight: bfloat16 [3072, 1024], replicated, may hold values from -0.109375 to 0.109375
- conv_bias: float32 [1024], replicated, may hold values from -1.75 to 1.75
- out_grad: bfloat16 [2, 8, 512, 1024], P(None, 'dp', 'ffn'), may hold values from -6 to 6
- comp_grad: bfloat16 [2, 8, 128, 1024], P(None, 'dp', 'ffn'), may hold values from -6 to 6
Outputs:
- layer_out: bfloat16 [2, 8, 512, 1024], P(None, 'dp', 'ffn')
- new_compressed: bfloat16 [2, 8, 128, 1024], P(None, 'dp', 'ffn')
- seg_grad: float32 [2, 8, 512, 1024], P(None, 'dp', 'ffn')
- attn_gain_grad: float32 [1024], replicated
- attn_shift_grad: float32 [1024], replicated
- attn_weights_grad: float32 [4096, 1024], P(('dp', 'ffn'))
- rel_table_grad: float32 [8, 22], replicated
- ffn_gain_grad: float32 [1024], replicated
- ffn_shift_grad: float32 [1024], replicated
- w_up_grad: float32 [1024, 4096], P('dp', 'ffn')
- b_up_grad: float32 [4096], replicated
- w_down_grad: float32 [4096, 1024], P('ffn', 'dp')
- b_down_grad: float32 [1024], replicated
- conv_weight_grad: float32 [3072, 1024], replicated
- conv_bias_grad: float32 [1024], replicated
Inputs may be any that keep to these rules, and one draw needn't show every extreme that they name: `mem_fill`: in every micro-batch one stream has all 384 memory slots live and another none; live slots are the newest, at the end of the buffer. `comp_fill`: in every micro-batch one stream has all 512 compressed slots live and another none; live slots are the newest, at the end of the buffer.
All inputs are finite; a program needn't handle non-finite values.
Results may differ from a plain program's by a relative error of at most 0.028.
Values may be sent and summed in bfloat16 or wider, within the bound.
No kernel may reach another device: no remote copies, remote signals or barrier semaphores. Data moves between devices by JAX's collectives and lax.ppermute only.
A program may use at most 320 MiB of HBM per device.

v0:
```python
import jax
import jax.numpy as jnp
from jax import lax
from jax.sharding import PartitionSpec as P

D = 1024
H = 8
HD = 128
M = 384
CM = 512
PW = 64
KR = 1408
NB = 22
EPSILON = 1e-05
MASKED_SCORE = -1e30


def normalize(rows_in, gain, shift):
    centre = jnp.mean(rows_in, axis=-1, keepdims=True)
    centred = rows_in - centre
    variance = jnp.mean(centred * centred, axis=-1, keepdims=True)
    return centred * lax.rsqrt(variance + EPSILON) * gain + shift


def smooth_unit(values_in):
    return jax.nn.gelu(values_in, approximate=False)


def matmul(left, right):
    return jnp.dot(left, right, preferred_element_type=jnp.float32)


def contract_rows(left, right):
    return lax.dot_general(
        left, right, (((0,), (0,)), ((), ())), preferred_element_type=jnp.float32
    )


def times_transposed(left, right):
    return lax.dot_general(
        left, right, (((1,), (1,)), ((), ())), preferred_element_type=jnp.float32
    )


def norm_backward(rows_in, gain, shift, cotangent):
    outputs, pullback = jax.vjp(normalize, rows_in, gain, shift)
    return pullback(cotangent)


def on_device(
    seg_input,
    memory,
    compressed,
    mem_fill,
    comp_fill,
    attn_gain,
    attn_shift,
    attn_weights,
    rel_table,
    ffn_gain,
    ffn_shift,
    w_up,
    b_up,
    w_down,
    b_down,
    conv_weight,
    conv_bias,
    out_grad,
    comp_grad,
):
    groups = lax.axis_size("ffn")
    ffn_rank = lax.axis_index("ffn")
    seg_rows = seg_input.shape[2]
    mem_rows = memory.shape[2]
    hidden_local = w_up.shape[1]
    query_tiles = seg_rows // PW
    score_scale = HD ** (-0.5)
    w_query = attn_weights[:D]
    w_key = attn_weights[D : 2 * D]
    w_value = attn_weights[2 * D : 3 * D]
    w_out = attn_weights[3 * D :]
    key_pos = jnp.arange(KR, dtype=jnp.int32)
    query_pos = CM + M + ffn_rank * seg_rows + jnp.arange(seg_rows, dtype=jnp.int32)
    query_blocks = (
        (CM + M) // PW + ffn_rank * query_tiles + jnp.arange(query_tiles, dtype=jnp.int32)
    )
    distance = query_blocks[:, None] - jnp.arange(NB, dtype=jnp.int32)[None, :]
    one_hot = (distance[:, :, None] == jnp.arange(NB, dtype=jnp.int32)[None, None, :]).astype(
        jnp.float32
    )
    tile_bias = jnp.einsum("hn,qkn->hqk", rel_table, one_hot, precision=lax.Precision.HIGHEST)
    memory_pos = ffn_rank * mem_rows + jnp.arange(mem_rows, dtype=jnp.int32)

    def scores_of(queries, key_heads, key_mask):
        raw_scores = (
            jnp.einsum("qhd,khd->hqk", queries, key_heads, preferred_element_type=jnp.float32)
            * score_scale
        )
        tiled = raw_scores.reshape(H, query_tiles, PW, NB, PW) + tile_bias[:, :, None, :, None]
        return jnp.where(key_mask[None], tiled.reshape(H, seg_rows, KR), MASKED_SCORE)

    def micro_batch(totals, sample):
        segment, memory_now, compressed_now, mem_count, comp_count, grad_rows_in, comp_cot = sample
        segment_f = segment.astype(jnp.float32)
        sources = (compressed_now.astype(jnp.float32), memory_now.astype(jnp.float32), segment_f)
        lowered = [
            normalize(section, attn_gain, attn_shift).astype(jnp.bfloat16) for section in sources
        ]
        own_keys = [matmul(section, w_key).astype(jnp.bfloat16) for section in lowered]
        own_values = [matmul(section, w_value).astype(jnp.bfloat16) for section in lowered]
        gathered = (
            lax.all_gather(own_keys[0], "ffn", axis=0, tiled=True),
            lax.all_gather(own_keys[1], "ffn", axis=0, tiled=True),
            lax.all_gather(own_keys[2], "ffn", axis=0, tiled=True),
            lax.all_gather(own_values[0], "ffn", axis=0, tiled=True),
            lax.all_gather(own_values[1], "ffn", axis=0, tiled=True),
            lax.all_gather(own_values[2], "ffn", axis=0, tiled=True),
        )
        key_heads = jnp.concatenate(gathered[:3], axis=0).reshape(KR, H, HD)
        value_heads = jnp.concatenate(gathered[3:], axis=0).reshape(KR, H, HD)
        queries = matmul(lowered[2], w_query).astype(jnp.bfloat16).reshape(seg_rows, H, HD)
        live_keys = jnp.where(
            key_pos < CM,
            key_pos >= CM - comp_count,
            jnp.where(key_pos < CM + M, key_pos >= CM + M - mem_count, True),
        )
        key_mask = live_keys[None, :] & (key_pos[None, :] <= query_pos[:, None])
        scores = scores_of(queries, key_heads, key_mask)
        row_max = jnp.max(scores, axis=-1, keepdims=True)
        expanded = jnp.exp(scores - row_max)
        row_total = jnp.sum(expanded, axis=-1, keepdims=True)
        log_total = row_max + jnp.log(row_total)
        attention = (expanded / row_total).astype(jnp.bfloat16)
        mixed_heads = jnp.einsum(
            "hqk,khd->qhd", attention, value_heads, preferred_element_type=jnp.float32
        )
        mixed_heads = mixed_heads.reshape(seg_rows, D).astype(jnp.bfloat16)
        residual = segment_f + matmul(mixed_heads, w_out)
        ffn_in = normalize(residual, ffn_gain, ffn_shift).astype(jnp.bfloat16)
        ffn_rows = lax.all_gather(ffn_in, "ffn", axis=0, tiled=True)
        hidden_pre = matmul(ffn_rows, w_up) + b_up
        activated_f, smooth_pull = jax.vjp(smooth_unit, hidden_pre)
        activated = activated_f.astype(jnp.bfloat16)
        branch = lax.psum_scatter(
            matmul(activated, w_down).astype(jnp.bfloat16), "ffn", scatter_dimension=0, tiled=True
        ).astype(jnp.float32)
        layer_rows = (residual + branch + b_down).astype(jnp.bfloat16)
        alive_rows = memory_pos >= M - mem_count
        flat_memory = jnp.where(
            alive_rows[:, None], memory_now, jnp.zeros_like(memory_now)
        ).reshape(mem_rows // 3, 3 * D)
        compressed_new = (matmul(flat_memory, conv_weight) + conv_bias).astype(jnp.bfloat16)
        grad_out = grad_rows_in.astype(jnp.float32)
        grad_all = lax.all_gather(grad_rows_in, "ffn", axis=0, tiled=True)
        grad_hidden = times_transposed(grad_all, w_down)
        grad_pre = smooth_pull(grad_hidden)[0].astype(jnp.bfloat16)
        down_grad = contract_rows(activated, grad_all)
        up_grad = contract_rows(ffn_rows, grad_pre)
        up_bias_part = jnp.sum(grad_pre.astype(jnp.float32), axis=0)
        grad_ffn_in = lax.psum_scatter(
            times_transposed(grad_pre, w_up).astype(jnp.bfloat16),
            "ffn",
            scatter_dimension=0,
            tiled=True,
        ).astype(jnp.float32)
        grad_normal, ffn_gain_part, ffn_shift_part = norm_backward(
            residual, ffn_gain, ffn_shift, grad_ffn_in
        )
        grad_residual = grad_out + grad_normal
        grad_branch = grad_residual.astype(jnp.bfloat16)
        out_weight_grad = contract_rows(mixed_heads, grad_branch)
        grad_mixed = (
            times_transposed(grad_branch, w_out).astype(jnp.bfloat16).reshape(seg_rows, H, HD)
        )
        scores_again = scores_of(queries, key_heads, key_mask)
        attention_f = jnp.exp(scores_again - log_total)
        grad_attention = jnp.einsum(
            "qhd,khd->hqk", grad_mixed, value_heads, preferred_element_type=jnp.float32
        )
        row_inner = jnp.sum(attention_f * grad_attention, axis=-1, keepdims=True)
        grad_scores = (attention_f * (grad_attention - row_inner)).astype(jnp.bfloat16)
        tile_grad = jnp.sum(
            grad_scores.astype(jnp.float32).reshape(H, query_tiles, PW, NB, PW), axis=(2, 4)
        )
        table_grad = jnp.einsum("hqk,qkn->hn", tile_grad, one_hot, precision=lax.Precision.HIGHEST)
        grad_query = (
            jnp.einsum("hqk,khd->qhd", grad_scores, key_heads, preferred_element_type=jnp.float32)
            * score_scale
        )
        grad_query = grad_query.reshape(seg_rows, D).astype(jnp.bfloat16)
        key_part = (
            jnp.einsum(
                "hqk,qhd->khd", grad_scores, queries, preferred_element_type=jnp.float32
            ).reshape(KR, D)
            * score_scale
        )
        value_part = jnp.einsum(
            "hqk,qhd->khd",
            attention_f.astype(jnp.bfloat16),
            grad_mixed,
            preferred_element_type=jnp.float32,
        ).reshape(KR, D)
        own_grads = (
            lax.psum_scatter(
                key_part[:CM].astype(jnp.bfloat16), "ffn", scatter_dimension=0, tiled=True
            ).astype(jnp.float32),
            lax.psum_scatter(
                key_part[CM : CM + M].astype(jnp.bfloat16), "ffn", scatter_dimension=0, tiled=True
            ).astype(jnp.float32),
            lax.psum_scatter(
                key_part[CM + M :].astype(jnp.bfloat16), "ffn", scatter_dimension=0, tiled=True
            ).astype(jnp.float32),
            lax.psum_scatter(
                value_part[:CM].astype(jnp.bfloat16), "ffn", scatter_dimension=0, tiled=True
            ).astype(jnp.float32),
            lax.psum_scatter(
                value_part[CM : CM + M].astype(jnp.bfloat16), "ffn", scatter_dimension=0, tiled=True
            ).astype(jnp.float32),
            lax.psum_scatter(
                value_part[CM + M :].astype(jnp.bfloat16), "ffn", scatter_dimension=0, tiled=True
            ).astype(jnp.float32),
        )
        grad_keys = [section.astype(jnp.bfloat16) for section in own_grads[:3]]
        grad_values = [section.astype(jnp.bfloat16) for section in own_grads[3:]]
        grad_normed = [
            times_transposed(grad_keys[section_id], w_key)
            + times_transposed(grad_values[section_id], w_value)
            for section_id in range(3)
        ]
        grad_normed[2] = grad_normed[2] + times_transposed(grad_query, w_query)
        query_weight_grad = contract_rows(lowered[2], grad_query)
        key_weight_grad = (
            contract_rows(lowered[0], grad_keys[0])
            + contract_rows(lowered[1], grad_keys[1])
            + contract_rows(lowered[2], grad_keys[2])
        )
        value_weight_grad = (
            contract_rows(lowered[0], grad_values[0])
            + contract_rows(lowered[1], grad_values[1])
            + contract_rows(lowered[2], grad_values[2])
        )
        norm_parts = [
            norm_backward(sources[section_id], attn_gain, attn_shift, grad_normed[section_id])
            for section_id in range(3)
        ]
        grad_segment = grad_residual + norm_parts[2][0]
        attn_gain_part = norm_parts[0][1] + norm_parts[1][1] + norm_parts[2][1]
        attn_shift_part = norm_parts[0][2] + norm_parts[1][2] + norm_parts[2][2]
        conv_grad = contract_rows(flat_memory, comp_cot)
        conv_bias_part = jnp.sum(comp_cot.astype(jnp.float32), axis=0)
        down_bias_part = jnp.sum(grad_out, axis=0)
        updates = (
            attn_gain_part,
            attn_shift_part,
            query_weight_grad,
            key_weight_grad,
            value_weight_grad,
            out_weight_grad,
            table_grad,
            ffn_gain_part,
            ffn_shift_part,
            up_grad,
            up_bias_part,
            down_grad,
            down_bias_part,
            conv_grad,
            conv_bias_part,
        )
        totals = jax.tree.map(jnp.add, totals, updates)
        return (totals, (layer_rows, compressed_new, grad_segment))

    float_zero = jnp.float32
    zero_grads = (
        jnp.zeros((D,), float_zero),
        jnp.zeros((D,), float_zero),
        jnp.zeros((D, D), float_zero),
        jnp.zeros((D, D), float_zero),
        jnp.zeros((D, D), float_zero),
        jnp.zeros((D, D), float_zero),
        jnp.zeros(rel_table.shape, float_zero),
        jnp.zeros((D,), float_zero),
        jnp.zeros((D,), float_zero),
        jnp.zeros(w_up.shape, float_zero),
        jnp.zeros((hidden_local,), float_zero),
        jnp.zeros(w_down.shape, float_zero),
        jnp.zeros((D,), float_zero),
        jnp.zeros(conv_weight.shape, float_zero),
        jnp.zeros((D,), float_zero),
    )
    samples = (
        seg_input[:, 0],
        memory[:, 0],
        compressed[:, 0],
        mem_fill[:, 0],
        comp_fill[:, 0],
        out_grad[:, 0],
        comp_grad[:, 0],
    )
    totals, stacked = lax.scan(micro_batch, zero_grads, samples)
    attn_grad = jnp.concatenate([totals[2], totals[3], totals[4], totals[5]], axis=0)
    attn_grad = lax.psum_scatter(attn_grad, ("dp", "ffn"), scatter_dimension=0, tiled=True)
    up_weight_grad, down_weight_grad = (
        lax.psum_scatter(totals[9], "dp", scatter_dimension=0, tiled=True),
        lax.psum_scatter(totals[11], "dp", scatter_dimension=1, tiled=True),
    )
    up_bias_full = lax.dynamic_update_slice(
        jnp.zeros((hidden_local * groups,), jnp.float32), totals[10], (ffn_rank * hidden_local,)
    )
    shared = lax.psum(
        (
            totals[13],
            totals[14],
            totals[0],
            totals[1],
            totals[7],
            totals[8],
            totals[12],
            totals[6],
            up_bias_full,
        ),
        ("dp", "ffn"),
    )
    return (
        stacked[0][:, None],
        stacked[1][:, None],
        stacked[2][:, None],
        shared[2],
        shared[3],
        attn_grad,
        shared[7],
        shared[4],
        shared[5],
        up_weight_grad,
        shared[8],
        down_weight_grad,
        shared[6],
        shared[0],
        shared[1],
    )


def solution(mesh):
    return jax.shard_map(
        on_device,
        mesh=mesh,
        in_specs=(
            P(None, "dp", "ffn", None),
            P(None, "dp", "ffn", None),
            P(None, "dp", "ffn", None),
            P(None, "dp"),
            P(None, "dp"),
            P(),
            P(),
            P(),
            P(),
            P(),
            P(),
            P(None, "ffn"),
            P("ffn"),
            P("ffn", None),
            P(),
            P(),
            P(),
            P(None, "dp", "ffn", None),
            P(None, "dp", "ffn", None),
        ),
        out_specs=(
            P(None, "dp", "ffn", None),
            P(None, "dp", "ffn", None),
            P(None, "dp", "ffn", None),
            P(),
            P(),
            P(("dp", "ffn"), None),
            P(),
            P(),
            P(),
            P("dp", "ffn"),
            P(),
            P("ffn", "dp"),
            P(),
            P(),
            P(),
        ),
        check_vma=False,
    )
```

profile of v0, /device:TPU:0, one launch (start us, length us, event | category | flops | bytes accessed | tf_op | source)
XLA Modules:
  0.0 1478.6 jit_solution(13740428444911833908)
XLA Ops:
  15.3 883.2 %while.46 = (s32[]{:T(128)}, f32[1024]{0:T(1024)}, f32[1024]{0:T(1024)}, f32[1024,1024]{1,0:T(8,128)}, f32[1024,1024]{1,0:T(8,128)}, /*index=5*/f32[1024,1024]{1...) while((s32[]{:T(128)}, f32[1024]{0:T(1024)}, ...), condition=%wide.region_36.37_spmd.clone.clone, body=%wide.region_0.36_spmd.clone.clone.sunk | while | flops 15250011136 | bytes 700114752 | solution.py:299
  27.5 31.8 %all_gather.47 = bf16[384,1024]{1,0:T(8,128)(2,1)} all-gather(bf16[96,1024]{1,0:T(8,128)(2,1)S(1)} %convolution_convert_fusion.23), channel_id=1, replica_groups=mesh['dp'=8,'ffn'=4] {'ffn'}, dimensions={0}, use_global_device_ids=true | all-gather | bytes 983040 | tf_op jit(solution)/shard_map/while/body/eval_jaxpr/all_gather | solution.py:113
  67.8 11.7 add.700
  87.2 21.5 %all_gather.50 = bf16[384,1024]{1,0:T(8,128)(2,1)} all-gather(bf16[96,1024]{1,0:T(8,128)(2,1)S(1)} %convolution_convert_fusion.26), channel_id=1, replica_groups=mesh['dp'=8,'ffn'=4] {'ffn'}, dimensions={0}, use_global_device_ids=true | all-gather | bytes 983040 | tf_op jit(solution)/shard_map/while/body/eval_jaxpr/all_gather | solution.py:116
  125.5 26.4 %all-gather.17.cloned.1.call-done = bf16[512,1024]{1,0:T(8,128)(2,1)} async-done(((bf16[128,1024]{1,0:T(8,128)(2,1)}), bf16[512,1024]{1,0:T(8,128)(2,1)}) %all-gather.17.cloned.1.call-update) | async-done | bytes 1048592 | tf_op jit(solution)/shard_map/while/body/eval_jaxpr/all_gather | solution.py:115
  162.1 24.7 %all-gather.19.cloned.1.call-done = bf16[512,1024]{1,0:T(8,128)(2,1)} async-done(((bf16[128,1024]{1,0:T(8,128)(2,1)}), bf16[512,1024]{1,0:T(8,128)(2,1)}) %all-gather.19.cloned.1.call-update) | async-done | bytes 1048592 | tf_op jit(solution)/shard_map/while/body/eval_jaxpr/all_gather | solution.py:140
  186.7 8.7 multiply_convert_fusion.5
  195.4 20.8 %all-gather.21.cloned.1.call-done = bf16[1,512,1024]{2,1,0:T(8,128)(2,1)} async-done(((bf16[1,128,1024]{2,1,0:T(8,128)(2,1)}), bf16[1,512,1024]{2,1,0:T(8,128)(2,1)}) %all-gather.21.cloned.1.call-update) | async-done | bytes 1048592 | tf_op jit(solution)/shard_map/while/body/eval_jaxpr/all_gather | solution.py:154
  229.6 22.5 %reduce-scatter.42.cloned.1.call-done = bf16[128,1024]{1,0:T(8,128)(2,1)} async-done(((bf16[512,1024]{1,0:T(8,128)(2,1)}), bf16[128,1024]{1,0:T(8,128)(2,1)}) %reduce-scatter.42.cloned.1.call-update) | async-done | bytes 262160 | tf_op jit(solution)/shard_map/while/body/eval_jaxpr/reduce_scatter | solution.py:160
  328.8 11.9 reshape.355
  340.7 10.8 reduce_sum.432
  376.1 10.1 reduce-scatter.46.cloned.1.call-done
  392.4 21.9 %reduce-scatter.48.cloned.1.call-done = bf16[128,1024]{1,0:T(8,128)(2,1)} async-done(((bf16[512,1024]{1,0:T(8,128)(2,1)}), bf16[128,1024]{1,0:T(8,128)(2,1)}) %reduce-scatter.48.cloned.1.call-update) | async-done | bytes 262160 | tf_op jit(solution)/shard_map/while
  416.9 25.5 %reduce-scatter.50.cloned.1.call-done = bf16[128,1024]{1,0:T(8,128)(2,1)} async-done(((bf16[512,1024]{1,0:T(8,128)(2,1)}), bf16[128,1024]{1,0:T(8,128)(2,1)}) %reduce-scatter.50.cloned.1.call-update) | async-done | bytes 262160 | tf_op jit(solution)/shard_map/while
  469.7 30.1 %all_gather.47 = bf16[384,1024]{1,0:T(8,128)(2,1)} all-gather(bf16[96,1024]{1,0:T(8,128)(2,1)S(1)} %convolution_convert_fusion.23), channel_id=1, replica_groups=mesh['dp'=8,'ffn'=4] {'ffn'}, dimensions={0}, use_global_device_ids=true | all-gather | bytes 983040 | tf_op jit(solution)/shard_map/while/body/eval_jaxpr/all_gather | solution.py:113
  508.4 11.7 add.700
  527.8 20.5 %all_gather.50 = bf16[384,1024]{1,0:T(8,128)(2,1)} all-gather(bf16[96,1024]{1,0:T(8,128)(2,1)S(1)} %convolution_convert_fusion.26), channel_id=1, replica_groups=mesh['dp'=8,'ffn'=4] {'ffn'}, dimensions={0}, use_global_device_ids=true | all-gather | bytes 983040 | tf_op jit(solution)/shard_map/while/body/eval_jaxpr/all_gather | solution.py:116
  565.1 24.6 %all-gather.17.cloned.1.call-done = bf16[512,1024]{1,0:T(8,128)(2,1)} async-done(((bf16[128,1024]{1,0:T(8,128)(2,1)}), bf16[512,1024]{1,0:T(8,128)(2,1)}) %all-gather.17.cloned.1.call-update) | async-done | bytes 1048592 | tf_op jit(solution)/shard_map/while/body/eval_jaxpr/all_gather | solution.py:115
  599.6 25.0 %all-gather.19.cloned.1.call-done = bf16[512,1024]{1,0:T(8,128)(2,1)} async-done(((bf16[128,1024]{1,0:T(8,128)(2,1)}), bf16[512,1024]{1,0:T(8,128)(2,1)}) %all-gather.19.cloned.1.call-update) | async-done | bytes 1048592 | tf_op jit(solution)/shard_map/while/body/eval_jaxpr/all_gather | solution.py:140
  624.6 8.7 multiply_convert_fusion.5
  633.3 20.8 %all-gather.21.cloned.1.call-done = bf16[1,512,1024]{2,1,0:T(8,128)(2,1)} async-done(((bf16[1,128,1024]{2,1,0:T(8,128)(2,1)}), bf16[1,512,1024]{2,1,0:T(8,128)(2,1)}) %all-gather.21.cloned.1.call-update) | async-done | bytes 1048592 | tf_op jit(solution)/shard_map/while/body/eval_jaxpr/all_gather | solution.py:154
  667.5 22.5 %reduce-scatter.42.cloned.1.call-done = bf16[128,1024]{1,0:T(8,128)(2,1)} async-done(((bf16[512,1024]{1,0:T(8,128)(2,1)}), bf16[128,1024]{1,0:T(8,128)(2,1)}) %reduce-scatter.42.cloned.1.call-update) | async-done | bytes 262160 | tf_op jit(solution)/shard_map/while/body/eval_jaxpr/reduce_scatter | solution.py:160
  741.8 11.2 select_add_fusion.35
  774.8 11.9 reshape.355
  786.7 11.0 reduce_sum.432
  832.1 20.0 %reduce-scatter.48.cloned.1.call-done = bf16[128,1024]{1,0:T(8,128)(2,1)} async-done(((bf16[512,1024]{1,0:T(8,128)(2,1)}), bf16[128,1024]{1,0:T(8,128)(2,1)}) %reduce-scatter.48.cloned.1.call-update) | async-done | bytes 262160 | tf_op jit(solution)/shard_map/while
  854.7 25.6 %reduce-scatter.50.cloned.1.call-done = bf16[128,1024]{1,0:T(8,128)(2,1)} async-done(((bf16[512,1024]{1,0:T(8,128)(2,1)}), bf16[128,1024]{1,0:T(8,128)(2,1)}) %reduce-scatter.50.cloned.1.call-update) | async-done | bytes 262160 | tf_op jit(solution)/shard_map/while
  900.5 12.7 pad_maximum_fusion.1
  914.1 40.6 %all-reduce = (f32[1024]{0:T(1024)}, f32[1024]{0:T(1024)}, f32[8,22]{1,0:T(8,128)}, f32[1024]{0:T(1024)}, f32[1024]{0:T(1024)}, /*index=5*/f32[4096]{0:T(1024)}, f32[1024]{0:T(1024)}, f32[1024]{0:T(1024)}) all-reduce(f32[1024]{0:T(1024)S(1)} %copy-done.75, f32[1024]{0:T(1024)S(1)} %copy-done.78, ...), channel_id=1, replica_groups=mesh['dp'=8,'ffn'=4] {'dp','ffn'}, use_global_device_ids=true, to_apply=%region_37.38 | all-reduce | flops 10416 | bytes 83328 | tf_op jit(solution)/shard_map/psum | solution.py:309
  954.8 400.1 %all-reduce.3.cloned.1.call-done = f32[3072,1024]{1,0:T(8,128)} async-done(((f32[3072,1024]{1,0:T(8,128)}), f32[3072,1024]{1,0:T(8,128)}) %all-reduce.3.cloned.1.call-update) | async-done | bytes 12582928 | tf_op jit(solution)/shard_map/psum | solution.py:309
  1354.8 104.0 %reduce-scatter.36.cloned.1.call-done = f32[128,1024]{1,0:T(8,128)} async-done(((f32[4096,1024]{1,0:T(8,128)}), f32[128,1024]{1,0:T(8,128)}) %reduce-scatter.36.cloned.1.call-update) | async-done | bytes 524304 | tf_op jit(solution)/shard_map/reduce_scatter | solution.py:301
  1458.8 12.1 copy.190
  (685 shorter events, 391.0 us)
Async XLA Ops:
  15.6 93.1 %all-gather.11.cloned.1.call-start = ((), (), s32[]{:S(2)}) async-start(), calls=%async_computation.15 | async-start | bytes 1310720 | tf_op jit(solution)/shard_map/while/body/eval_jaxpr/all_gather | solution.py:114
  17.3 91.4 %all-gather.13.cloned.1.call-start = ((), (), s32[]{:S(2)}) async-start(), calls=%async_computation.16 | async-start | bytes 1310720 | tf_op jit(solution)/shard_map/while/body/eval_jaxpr/all_gather | solution.py:112
  19.0 106.5 %all-gather.15.cloned.1.call-start = ((), (), s32[]{:S(2)}) async-start(), calls=%async_computation.17 | async-start | bytes 1310720 | tf_op jit(solution)/shard_map/while/body/eval_jaxpr/all_gather | solution.py:117
  22.0 129.9 %all-gather.17.cloned.1.call-start = ((), (), s32[]{:S(2)}) async-start(), calls=%async_computation.18 | async-start | bytes 1310720 | tf_op jit(solution)/shard_map/while/body/eval_jaxpr/all_gather | solution.py:115
  24.9 161.8 %all-gather.19.cloned.1.call-start = ((), (), s32[]{:S(2)}) async-start(), calls=%async_computation.19 | async-start | bytes 1310720 | tf_op jit(solution)/shard_map/while/body/eval_jaxpr/all_gather | solution.py:140
  159.1 57.0 %all-gather.21.cloned.1.call-start = ((), (), s32[]{:S(2)}) async-start(), calls=%async_computation.20 | async-start | bytes 1310720 | tf_op jit(solution)/shard_map/while/body/eval_jaxpr/all_gather | solution.py:154
  161.5 90.6 %reduce-scatter.42.cloned.1.call-start = ((), (), s32[]{:S(2)}) async-start(), calls=%async_computation.21 | async-start | bytes 1310720 | tf_op jit(solution)/shard_map/while/body/eval_jaxpr/reduce_scatter | solution.py:160
  225.3 137.8 %reduce-scatter.56.cloned.1.call-start = ((), (), s32[]{:S(2)}) async-start(), calls=%async_computation.28 | async-start | bytes 1310720 | tf_op jit(solution)/shard_map/while/body/eval_jaxpr/reduce_scatter | solution.py:144
  229.6 135.3 %reduce-scatter.52.cloned.1.call-start = ((), (), s32[]{:S(2)}) async-start(), calls=%async_computation.26 | async-start | bytes 983040 | tf_op jit(solution)/shard_map/while
  274.1 95.4 %reduce-scatter.54.cloned.1.call-start = ((), (), s32[]{:S(2)}) async-start(), calls=%async_computation.27 | async-start | bytes 983040 | tf_op jit(solution)/shard_map/while
  283.1 91.2 %reduce-scatter.44.cloned.1.call-start = ((), (), s32[]{:S(2)}) async-start(), calls=%async_computation.22 | async-start | bytes 1310720 | tf_op jit(solution)/shard_map/while
  288.5 97.7 %reduce-scatter.46.cloned.1.call-start = ((), (), s32[]{:S(2)}) async-start(), calls=%async_computation.23 | async-start | bytes 1310720 | tf_op jit(solution)/shard_map/while
  294.0 120.3 %reduce-scatter.48.cloned.1.call-start = ((), (), s32[]{:S(2)}) async-start(), calls=%async_computation.24 | async-start | bytes 1310720 | tf_op jit(solution)/shard_map/while
  312.8 129.5 %reduce-scatter.50.cloned.1.call-start = ((), (), s32[]{:S(2)}) async-start(), calls=%async_computation.25 | async-start | bytes 1310720 | tf_op jit(solution)/shard_map/while
  457.8 90.5 %all-gather.11.cloned.1.call-start = ((), (), s32[]{:S(2)}) async-start(), calls=%async_computation.15 | async-start | bytes 1310720 | tf_op jit(solution)/shard_map/while/body/eval_jaxpr/all_gather | solution.py:114
  459.5 88.8 %all-gather.13.cloned.1.call-start = ((), (), s32[]{:S(2)}) async-start(), calls=%async_computation.16 | async-start | bytes 1310720 | tf_op jit(solution)/shard_map/while/body/eval_jaxpr/all_gather | solution.py:112
  461.2 103.9 %all-gather.15.cloned.1.call-start = ((), (), s32[]{:S(2)}) async-start(), calls=%async_computation.17 | async-start | bytes 1310720 | tf_op jit(solution)/shard_map/while/body/eval_jaxpr/all_gather | solution.py:117
  464.2 125.6 %all-gather.17.cloned.1.call-start = ((), (), s32[]{:S(2)}) async-start(), calls=%async_computation.18 | async-start | bytes 1310720 | tf_op jit(solution)/shard_map/while/body/eval_jaxpr/all_gather | solution.py:115
  467.1 157.5 %all-gather.19.cloned.1.call-start = ((), (), s32[]{:S(2)}) async-start(), calls=%async_computation.19 | async-start | bytes 1310720 | tf_op jit(solution)/shard_map/while/body/eval_jaxpr/all_gather | solution.py:140
  597.0 57.0 %all-gather.21.cloned.1.call-start = ((), (), s32[]{:S(2)}) async-start(), calls=%async_computation.20 | async-start | bytes 1310720 | tf_op jit(solution)/shard_map/while/body/eval_jaxpr/all_gather | solution.py:154
  599.4 90.6 %reduce-scatter.42.cloned.1.call-start = ((), (), s32[]{:S(2)}) async-start(), calls=%async_computation.21 | async-start | bytes 1310720 | tf_op jit(solution)/shard_map/while/body/eval_jaxpr/reduce_scatter | solution.py:160
  663.2 149.7 %reduce-scatter.56.cloned.1.call-start = ((), (), s32[]{:S(2)}) async-start(), calls=%async_computation.28 | async-start | bytes 1310720 | tf_op jit(solution)/shard_map/while/body/eval_jaxpr/reduce_scatter | solution.py:144
  667.4 147.2 %reduce-scatter.52.cloned.1.call-start = ((), (), s32[]{:S(2)}) async-start(), calls=%async_computation.26 | async-start | bytes 983040 | tf_op jit(solution)/shard_map/while
  712.0 107.3 %reduce-scatter.54.cloned.1.call-start = ((), (), s32[]{:S(2)}) async-start(), calls=%async_computation.27 | async-start | bytes 983040 | tf_op jit(solution)/shard_map/while
  721.0 103.1 %reduce-scatter.44.cloned.1.call-start = ((), (), s32[]{:S(2)}) async-start(), calls=%async_computation.22 | async-start | bytes 1310720 | tf_op jit(solution)/shard_map/while
  726.4 99.5 %reduce-scatter.46.cloned.1.call-start = ((), (), s32[]{:S(2)}) async-start(), calls=%async_computation.23 | async-start | bytes 1310720 | tf_op jit(solution)/shard_map/while
  731.9 120.2 %reduce-scatter.48.cloned.1.call-start = ((), (), s32[]{:S(2)}) async-start(), calls=%async_computation.24 | async-start | bytes 1310720 | tf_op jit(solution)/shard_map/while
  755.4 125.0 %reduce-scatter.50.cloned.1.call-start = ((), (), s32[]{:S(2)}) async-start(), calls=%async_computation.25 | async-start | bytes 1310720 | tf_op jit(solution)/shard_map/while
  898.5 456.3 %all-reduce.3.cloned.1.call-start = ((), (), s32[]{:S(2)}) async-start(), calls=%async_computation.14 | async-start | bytes 25165824 | tf_op jit(solution)/shard_map/psum | solution.py:309
  899.1 455.8 %reduce-scatter.38.cloned.1.call-start = ((), (), s32[]{:S(2)}) async-start(), calls=%async_computation.12 | async-start | bytes 4718592 | tf_op jit(solution)/shard_map/reduce_scatter | solution.py:303
  899.8 455.0 %reduce-scatter.40.cloned.1.call-start = ((), (), s32[]{:S(2)}) async-start(), calls=%async_computation.13 | async-start | bytes 4718592 | tf_op jit(solution)/shard_map/reduce_scatter | solution.py:304
  900.4 558.4 %reduce-scatter.36.cloned.1.call-start = ((), (), s32[]{:S(2)}) async-start(), calls=%async_computation.11 | async-start | bytes 17301504 | tf_op jit(solution)/shard_map/reduce_scatter | solution.py:301
  (185 other events, 1737.2 us)
Sparse Core Ops, SparseCore 0:
  18.6 43.2 all-gather.10
  63.5 27.4 all-gather.12
  92.6 30.4 all-gather.14
  124.4 27.3 all-gather.16
  159.2 27.4 all-gather.18
  188.7 27.4 all-gather.20
  225.4 26.6 reduce-scatter.41
  254.5 25.8 reduce-scatter.55
  282.7 21.9 reduce-scatter.51
  306.8 22.5 reduce-scatter.53
  331.7 26.4 reduce-scatter.43
  360.4 25.7 reduce-scatter.45
  388.5 25.7 reduce-scatter.47
  416.6 25.7 reduce-scatter.49
  460.5 39.7 all-gather.10
  501.7 26.9 all-gather.12
  530.1 30.8 all-gather.14
  562.5 27.2 all-gather.16
  597.1 27.4 all-gather.18
  626.6 27.4 all-gather.20
  663.3 26.6 reduce-scatter.41
  692.4 25.8 reduce-scatter.55
  720.6 21.9 reduce-scatter.51
  744.7 22.5 reduce-scatter.53
  769.6 26.4 reduce-scatter.43
  798.3 25.7 reduce-scatter.45
  826.3 25.7 reduce-scatter.47
  854.5 25.7 reduce-scatter.49
  903.9 51.9 reduce-scatter.37
  960.0 51.9 reduce-scatter.39
  1014.9 443.9 reduce-scatter.35
Sparse Core Ops, SparseCore 1:
  905.6 449.2 all-reduce.2
where the time goes:
time: 1480 us
  waiting for transfers between devices  797 us (54%)
  matrix products  233 us (16%)
  local copies, waits for them, and re-layouts  197 us (13%)
  blocking collectives  145 us (10%)
  other arithmetic  78.2 us (5%)
  between operations  16.1 us (1%)
    psum x1, waiting for transfers between devices, on_device(): lax.psum((totals[13], totals[14], totals[0], totals[1], totals[7], totals...  400 us
    reduce_scatter x1, waiting for transfers between devices, on_device(): lax.psum_scatter(attn_grad, ('dp', 'ffn'), scatter_dimension=0, tiled=True)  104 us
    while x40, waiting for transfers between devices  104 us
    dot_general x22, matrix products, contract_rows(): lax.dot_general(left, right, (((0,), (0,)), ((), ())), preferred_element_...  78.7 us
    all_gather x2, blocking collectives, micro_batch(): lax.all_gather(own_keys[1], 'ffn', axis=0, tiled=True)  61.9 us
    while x348, local copies, waits for them, and re-layouts  60.1 us
    dot_general x22, matrix products, matmul(): return jnp.dot(left, right, preferred_element_type=jnp.float32)  57.1 us
    all_gather x2, waiting for transfers between devices, micro_batch(): lax.all_gather(own_values[0], 'ffn', axis=0, tiled=True)  51 us
  transfers between devices with their start and end apart: 32, of which 15 were waited for; matrix products, arithmetic and copies ran while one was open for 28% of the time, Pallas kernels for 0%

commit v1 on v0

--- a/solution.py
+++ b/solution.py
@@ -151,7 +151,14 @@
         ).reshape(mem_rows // 3, 3 * D)
         compressed_new = (matmul(flat_memory, conv_weight) + conv_bias).astype(jnp.bfloat16)
         grad_out = grad_rows_in.astype(jnp.float32)
-        grad_all = lax.all_gather(grad_rows_in, "ffn", axis=0, tiled=True)
+        ring = [grad_rows_in]
+        for hop in range(3):
+            ring.append(lax.ppermute(ring[-1], "ffn", [(dev, (dev + 1) % 4) for dev in range(4)]))
+        grad_all = jnp.roll(
+            jnp.concatenate(ring[::-1], axis=0),
+            (lax.axis_index("ffn") + 1) * ring[0].shape[0],
+            axis=0,
+        )
         grad_hidden = times_transposed(grad_all, w_down)
         grad_pre = smooth_pull(grad_hidden)[0].astype(jnp.bfloat16)
         down_grad = contract_rows(activated, grad_all)

time: 1480 us -> 1480 us (level)
  waiting for transfers between devices: 797 us -> 749 us
  local copies, waits for them, and re-layouts: 197 us -> 225 us
    all_gather x2, waiting for transfers between devices: 49.7 us -> 0.01 us  [micro_batch(): ffn_rows = lax.all_gather(ffn_in, 'ffn', axis=0, tiled=True)]
    ppermute x0 -> x6, waiting for transfers between devices: none -> 49.4 us  [micro_batch(): lax.ppermute(ring[-1], 'ffn', [(dev, (dev + 1) % 4) for dev in range(4)])]
    all_gather x2 -> x0, waiting for transfers between devices: 41.5 us -> none  [micro_batch(): grad_all = lax.all_gather(grad_rows_in, 'ffn', axis=0, tiled=True)]
    while x348 -> x354, local copies, waits for them, and re-layouts: 60.1 us -> 83.9 us
    while x40 -> x38, waiting for transfers between devices: 104 us -> 101 us
  transfers between devices with their start and end apart: 32 -> 36, of which waited for: 15 -> 15; matrix products, arithmetic and copies ran while one was open for 28% -> 30% of each run, Pallas kernels for 0% -> 0%
where the time goes in v1:
time: 1480 us; the launch traced here: 1470 us
  waiting for transfers between devices  749 us (51%)
  matrix products  226 us (15%)
  local copies, waits for them, and re-layouts  225 us (15%)
  blocking collectives  155 us (10%)
  other arithmetic  82.9 us (6%)
  between operations  15.8 us (1%)
    psum x1, waiting for transfers between devices, on_device(): lax.psum((totals[13], totals[14], totals[0], totals[1], totals[7], totals...  400 us
    reduce_scatter x1, waiting for transfers between devices, on_device(): lax.psum_scatter(attn_grad, ('dp', 'ffn'), scatter_dimension=0, tiled=True)  104 us
    while x38, waiting for transfers between devices  101 us
    while x354, local copies, waits for them, and re-layouts  83.9 us
    dot_general x22, matrix products, contract_rows(): lax.dot_general(left, right, (((0,), (0,)), ((), ())), preferred_element_...  78.6 us
    all_gather x2, blocking collectives, micro_batch(): lax.all_gather(own_keys[1], 'ffn', axis=0, tiled=True)  68.6 us
    dot_general x22, matrix products, matmul(): return jnp.dot(left, right, preferred_element_type=jnp.float32)  56.1 us
    reduce_scatter x2, waiting for transfers between devices, micro_batch(): lax.psum_scatter(times_transposed(grad_pre, w_up).astype(jnp.bfloat16), '...  50.4 us
  transfers between devices with their start and end apart: 36, of which 15 were waited for; matrix products, arithmetic and copies ran while one was open for 30% of the time, Pallas kernels for 0%

profile of v1, /device:TPU:0, one launch (start us, length us, event | category | flops | bytes accessed | tf_op | source)
XLA Modules:
  0.0 1472.2 jit_solution(10151193946812937605)
XLA Ops:
  15.3 876.9 %while.48 = (s32[]{:T(128)}, f32[1024]{0:T(1024)}, f32[1024]{0:T(1024)}, f32[1024,1024]{1,0:T(8,128)}, f32[1024,1024]{1,0:T(8,128)}, /*index=5*/f32[1024,1024]{1...) while((s32[]{:T(128)}, f32[1024]{0:T(1024)}, ...), condition=%wide.region_36.37_spmd.clone.clone, body=%wide.region_0.36_spmd.clone.clone.sunk | while | flops 15250011136 | bytes 711862336 | solution.py:306
  32.7 34.9 %all_gather.64 = bf16[384,1024]{1,0:T(8,128)(2,1)} all-gather(bf16[96,1024]{1,0:T(8,128)(2,1)S(1)} %convolution_convert_fusion.23), channel_id=1, replica_groups=mesh['dp'=8,'ffn'=4] {'ffn'}, dimensions={0}, use_global_device_ids=true | all-gather | bytes 983040 | tf_op jit(solution)/shard_map/while/body/eval_jaxpr/all_gather | solution.py:113
  76.2 11.7 add.894
  95.6 22.9 %all_gather.67 = bf16[384,1024]{1,0:T(8,128)(2,1)} all-gather(bf16[96,1024]{1,0:T(8,128)(2,1)S(1)} %convolution_convert_fusion.26), channel_id=1, replica_groups=mesh['dp'=8,'ffn'=4] {'ffn'}, dimensions={0}, use_global_device_ids=true | all-gather | bytes 983040 | tf_op jit(solution)/shard_map/while/body/eval_jaxpr/all_gather | solution.py:116
  135.3 20.3 %all-gather.12.cloned.1.call-done = bf16[512,1024]{1,0:T(8,128)(2,1)} async-done(((bf16[128,1024]{1,0:T(8,128)(2,1)}), bf16[512,1024]{1,0:T(8,128)(2,1)}) %all-gather.12.cloned.1.call-update) | async-done | bytes 1048592 | tf_op jit(solution)/shard_map/while/body/eval_jaxpr/all_gather | solution.py:115
  164.4 8.6 collective-permute-done.1
  173.6 16.1 %collective-permute-done.2 = bf16[128,1024]{1,0:T(8,128)(2,1)} collective-permute-done((bf16[128,1024]{1,0:T(8,128)(2,1)}, bf16[128,1024]{1,0:T(8,128)(2,1)}, u32[]{:S(2)}, u32[]{:S(2)}) %collective-permute-start.2) | collective-permute-done | bytes 262176 | tf_op jit(solution)/shard_map/while/body/eval_jaxpr/ppermute | solution.py:156
  203.1 8.2 multiply_convert_fusion.5
  222.9 25.1 %reduce-scatter.42.cloned.1.call-done = bf16[128,1024]{1,0:T(8,128)(2,1)} async-done(((bf16[512,1024]{1,0:T(8,128)(2,1)}), bf16[128,1024]{1,0:T(8,128)(2,1)}) %reduce-scatter.42.cloned.1.call-update) | async-done | bytes 262160 | tf_op jit(solution)/shard_map/while/body/eval_jaxpr/reduce_scatter | solution.py:167
  326.1 11.9 reshape.423
  338.0 10.8 reduce_sum.510
  373.4 8.8 reduce-scatter.46.cloned.1.call-done
  388.5 21.8 %reduce-scatter.48.cloned.1.call-done = bf16[128,1024]{1,0:T(8,128)(2,1)} async-done(((bf16[512,1024]{1,0:T(8,128)(2,1)}), bf16[128,1024]{1,0:T(8,128)(2,1)}) %reduce-scatter.48.cloned.1.call-update) | async-done | bytes 262160 | tf_op jit(solution)/shard_map/while
  412.8 25.6 %reduce-scatter.50.cloned.1.call-done = bf16[128,1024]{1,0:T(8,128)(2,1)} async-done(((bf16[512,1024]{1,0:T(8,128)(2,1)}), bf16[128,1024]{1,0:T(8,128)(2,1)}) %reduce-scatter.50.cloned.1.call-update) | async-done | bytes 262160 | tf_op jit(solution)/shard_map/while
  468.1 33.8 %all_gather.64 = bf16[384,1024]{1,0:T(8,128)(2,1)} all-gather(bf16[96,1024]{1,0:T(8,128)(2,1)S(1)} %convolution_convert_fusion.23), channel_id=1, replica_groups=mesh['dp'=8,'ffn'=4] {'ffn'}, dimensions={0}, use_global_device_ids=true | all-gather | bytes 983040 | tf_op jit(solution)/shard_map/while/body/eval_jaxpr/all_gather | solution.py:113
  510.4 11.6 add.894
  529.8 23.2 %all_gather.67 = bf16[384,1024]{1,0:T(8,128)(2,1)} all-gather(bf16[96,1024]{1,0:T(8,128)(2,1)S(1)} %convolution_convert_fusion.26), channel_id=1, replica_groups=mesh['dp'=8,'ffn'=4] {'ffn'}, dimensions={0}, use_global_device_ids=true | all-gather | bytes 983040 | tf_op jit(solution)/shard_map/while/body/eval_jaxpr/all_gather | solution.py:116
  569.8 21.8 %all-gather.12.cloned.1.call-done = bf16[512,1024]{1,0:T(8,128)(2,1)} async-done(((bf16[128,1024]{1,0:T(8,128)(2,1)}), bf16[512,1024]{1,0:T(8,128)(2,1)}) %all-gather.12.cloned.1.call-update) | async-done | bytes 1048592 | tf_op jit(solution)/shard_map/while/body/eval_jaxpr/all_gather | solution.py:115
  600.4 8.6 collective-permute-done.1
  609.2 16.1 %collective-permute-done.2 = bf16[128,1024]{1,0:T(8,128)(2,1)} collective-permute-done((bf16[128,1024]{1,0:T(8,128)(2,1)}, bf16[128,1024]{1,0:T(8,128)(2,1)}, u32[]{:S(2)}, u32[]{:S(2)}) %collective-permute-start.2) | collective-permute-done | bytes 262176 | tf_op jit(solution)/shard_map/while/body/eval_jaxpr/ppermute | solution.py:156
  638.8 8.2 multiply_convert_fusion.5
  658.5 25.3 %reduce-scatter.42.cloned.1.call-done = bf16[128,1024]{1,0:T(8,128)(2,1)} async-done(((bf16[512,1024]{1,0:T(8,128)(2,1)}), bf16[128,1024]{1,0:T(8,128)(2,1)}) %reduce-scatter.42.cloned.1.call-update) | async-done | bytes 262160 | tf_op jit(solution)/shard_map/while/body/eval_jaxpr/reduce_scatter | solution.py:167
  737.1 11.2 select_add_fusion.36
  770.2 11.9 reshape.423
  782.1 11.0 reduce_sum.510
  827.4 18.6 %reduce-scatter.48.cloned.1.call-done = bf16[128,1024]{1,0:T(8,128)(2,1)} async-done(((bf16[512,1024]{1,0:T(8,128)(2,1)}), bf16[128,1024]{1,0:T(8,128)(2,1)}) %reduce-scatter.48.cloned.1.call-update) | async-done | bytes 262160 | tf_op jit(solution)/shard_map/while
  848.5 25.5 %reduce-scatter.50.cloned.1.call-done = bf16[128,1024]{1,0:T(8,128)(2,1)} async-done(((bf16[512,1024]{1,0:T(8,128)(2,1)}), bf16[128,1024]{1,0:T(8,128)(2,1)}) %reduce-scatter.50.cloned.1.call-update) | async-done | bytes 262160 | tf_op jit(solution)/shard_map/while
  894.2 12.8 pad_maximum_fusion.1
  907.9 40.6 %all-reduce = (f32[1024]{0:T(1024)}, f32[1024]{0:T(1024)}, f32[8,22]{1,0:T(8,128)}, f32[1024]{0:T(1024)}, f32[1024]{0:T(1024)}, /*index=5*/f32[4096]{0:T(1024)}, f32[1024]{0:T(1024)}, f32[1024]{0:T(1024)}) all-reduce(f32[1024]{0:T(1024)S(1)} %copy-done.72, f32[1024]{0:T(1024)S(1)} %copy-done.75, ...), channel_id=1, replica_groups=mesh['dp'=8,'ffn'=4] {'dp','ffn'}, use_global_device_ids=true, to_apply=%region_37.38 | all-reduce | flops 10416 | bytes 83328 | tf_op jit(solution)/shard_map/psum | solution.py:316
  948.5 400.2 %all-reduce.3.cloned.1.call-done = f32[3072,1024]{1,0:T(8,128)} async-done(((f32[3072,1024]{1,0:T(8,128)}), f32[3072,1024]{1,0:T(8,128)}) %all-reduce.3.cloned.1.call-update) | async-done | bytes 12582928 | tf_op jit(solution)/shard_map/psum | solution.py:316
  1348.7 104.0 %reduce-scatter.36.cloned.1.call-done = f32[128,1024]{1,0:T(8,128)} async-done(((f32[4096,1024]{1,0:T(8,128)}), f32[128,1024]{1,0:T(8,128)}) %reduce-scatter.36.cloned.1.call-update) | async-done | bytes 524304 | tf_op jit(solution)/shard_map/reduce_scatter | solution.py:308
  1452.7 12.1 copy.197
  (701 shorter events, 422.7 us)
Async XLA Ops:
  15.6 103.0 %all-gather.6.cloned.1.call-start = ((), (), s32[]{:S(2)}) async-start(), calls=%async_computation.15 | async-start | bytes 1310720 | tf_op jit(solution)/shard_map/while/body/eval_jaxpr/all_gather | solution.py:114
  17.2 101.3 %all-gather.8.cloned.1.call-start = ((), (), s32[]{:S(2)}) async-start(), calls=%async_computation.16 | async-start | bytes 1310720 | tf_op jit(solution)/shard_map/while/body/eval_jaxpr/all_gather | solution.py:112
  18.9 116.4 %all-gather.10.cloned.1.call-start = ((), (), s32[]{:S(2)}) async-start(), calls=%async_computation.17 | async-start | bytes 1310720 | tf_op jit(solution)/shard_map/while/body/eval_jaxpr/all_gather | solution.py:117
  21.8 133.8 %all-gather.12.cloned.1.call-start = ((), (), s32[]{:S(2)}) async-start(), calls=%async_computation.18 | async-start | bytes 1310720 | tf_op jit(solution)/shard_map/while/body/eval_jaxpr/all_gather | solution.py:115
  24.2 138.8 %collective-permute-start = (bf16[128,1024]{1,0:T(8,128)(2,1)}, bf16[128,1024]{1,0:T(8,128)(2,1)}, u32[]{:S(2)}, u32[]{:S(2)}) collective-permute-start(bf16[128,1024]{1,0:T(8,128)(2,1)} %get-tuple-element.1430), channel_id=1, source_target_pairs={{0,1},{1,2},{2,3},{3,0},{4,5},{5,6},{6,7},{7,4},{8,9},{9,10},{10,1... | collective-permute-start | bytes 786440 | tf_op jit(solution)/shard_map/while/body/eval_jaxpr/ppermute | solution.py:156
  30.1 173.0 %all-gather.14.cloned.1.call-start = ((), (), s32[]{:S(2)}) async-start(), calls=%async_computation.19 | async-start | bytes 1310720 | tf_op jit(solution)/shard_map/while/body/eval_jaxpr/all_gather | solution.py:140
  162.9 85.1 %reduce-scatter.42.cloned.1.call-start = ((), (), s32[]{:S(2)}) async-start(), calls=%async_computation.20 | async-start | bytes 1310720 | tf_op jit(solution)/shard_map/while/body/eval_jaxpr/reduce_scatter | solution.py:167
  218.6 141.8 %reduce-scatter.56.cloned.1.call-start = ((), (), s32[]{:S(2)}) async-start(), calls=%async_computation.27 | async-start | bytes 1310720 | tf_op jit(solution)/shard_map/while/body/eval_jaxpr/reduce_scatter | solution.py:144
  222.9 139.4 %reduce-scatter.52.cloned.1.call-start = ((), (), s32[]{:S(2)}) async-start(), calls=%async_computation.25 | async-start | bytes 983040 | tf_op jit(solution)/shard_map/while
  270.0 96.8 %reduce-scatter.54.cloned.1.call-start = ((), (), s32[]{:S(2)}) async-start(), calls=%async_computation.26 | async-start | bytes 983040 | tf_op jit(solution)/shard_map/while
  279.0 92.7 %reduce-scatter.44.cloned.1.call-start = ((), (), s32[]{:S(2)}) async-start(), calls=%async_computation.21 | async-start | bytes 1310720 | tf_op jit(solution)/shard_map/while
  284.4 97.9 %reduce-scatter.46.cloned.1.call-start = ((), (), s32[]{:S(2)}) async-start(), calls=%async_computation.22 | async-start | bytes 1310720 | tf_op jit(solution)/shard_map/while
  289.9 120.4 %reduce-scatter.48.cloned.1.call-start = ((), (), s32[]{:S(2)}) async-start(), calls=%async_computation.23 | async-start | bytes 1310720 | tf_op jit(solution)/shard_map/while
  310.2 128.3 %reduce-scatter.50.cloned.1.call-start = ((), (), s32[]{:S(2)}) async-start(), calls=%async_computation.24 | async-start | bytes 1310720 | tf_op jit(solution)/shard_map/while
  453.9 99.1 %all-gather.6.cloned.1.call-start = ((), (), s32[]{:S(2)}) async-start(), calls=%async_computation.15 | async-start | bytes 1310720 | tf_op jit(solution)/shard_map/while/body/eval_jaxpr/all_gather | solution.py:114
  455.6 97.4 %all-gather.8.cloned.1.call-start = ((), (), s32[]{:S(2)}) async-start(), calls=%async_computation.16 | async-start | bytes 1310720 | tf_op jit(solution)/shard_map/while/body/eval_jaxpr/all_gather | solution.py:112
  457.3 112.5 %all-gather.10.cloned.1.call-start = ((), (), s32[]{:S(2)}) async-start(), calls=%async_computation.17 | async-start | bytes 1310720 | tf_op jit(solution)/shard_map/while/body/eval_jaxpr/all_gather | solution.py:117
  460.2 131.4 %all-gather.12.cloned.1.call-start = ((), (), s32[]{:S(2)}) async-start(), calls=%async_computation.18 | async-start | bytes 1310720 | tf_op jit(solution)/shard_map/while/body/eval_jaxpr/all_gather | solution.py:115
  462.6 136.4 %collective-permute-start = (bf16[128,1024]{1,0:T(8,128)(2,1)}, bf16[128,1024]{1,0:T(8,128)(2,1)}, u32[]{:S(2)}, u32[]{:S(2)}) collective-permute-start(bf16[128,1024]{1,0:T(8,128)(2,1)} %get-tuple-element.1430), channel_id=1, source_target_pairs={{0,1},{1,2},{2,3},{3,0},{4,5},{5,6},{6,7},{7,4},{8,9},{9,10},{10,1... | collective-permute-start | bytes 786440 | tf_op jit(solution)/shard_map/while/body/eval_jaxpr/ppermute | solution.py:156
  465.5 173.3 %all-gather.14.cloned.1.call-start = ((), (), s32[]{:S(2)}) async-start(), calls=%async_computation.19 | async-start | bytes 1310720 | tf_op jit(solution)/shard_map/while/body/eval_jaxpr/all_gather | solution.py:140
  598.9 84.9 %reduce-scatter.42.cloned.1.call-start = ((), (), s32[]{:S(2)}) async-start(), calls=%async_computation.20 | async-start | bytes 1310720 | tf_op jit(solution)/shard_map/while/body/eval_jaxpr/reduce_scatter | solution.py:167
  654.2 153.9 %reduce-scatter.56.cloned.1.call-start = ((), (), s32[]{:S(2)}) async-start(), calls=%async_computation.27 | async-start | bytes 1310720 | tf_op jit(solution)/shard_map/while/body/eval_jaxpr/reduce_scatter | solution.py:144
  658.5 151.4 %reduce-scatter.52.cloned.1.call-start = ((), (), s32[]{:S(2)}) async-start(), calls=%async_computation.25 | async-start | bytes 983040 | tf_op jit(solution)/shard_map/while
  705.8 108.7 %reduce-scatter.54.cloned.1.call-start = ((), (), s32[]{:S(2)}) async-start(), calls=%async_computation.26 | async-start | bytes 983040 | tf_op jit(solution)/shard_map/while
  714.8 104.5 %reduce-scatter.44.cloned.1.call-start = ((), (), s32[]{:S(2)}) async-start(), calls=%async_computation.21 | async-start | bytes 1310720 | tf_op jit(solution)/shard_map/while
  720.3 100.8 %reduce-scatter.46.cloned.1.call-start = ((), (), s32[]{:S(2)}) async-start(), calls=%async_computation.22 | async-start | bytes 1310720 | tf_op jit(solution)/shard_map/while
  725.8 120.2 %reduce-scatter.48.cloned.1.call-start = ((), (), s32[]{:S(2)}) async-start(), calls=%async_computation.23 | async-start | bytes 1310720 | tf_op jit(solution)/shard_map/while
  750.6 123.4 %reduce-scatter.50.cloned.1.call-start = ((), (), s32[]{:S(2)}) async-start(), calls=%async_computation.24 | async-start | bytes 1310720 | tf_op jit(solution)/shard_map/while
  892.2 456.5 %all-reduce.3.cloned.1.call-start = ((), (), s32[]{:S(2)}) async-start(), calls=%async_computation.14 | async-start | bytes 25165824 | tf_op jit(solution)/shard_map/psum | solution.py:316
  892.8 455.9 %reduce-scatter.38.cloned.1.call-start = ((), (), s32[]{:S(2)}) async-start(), calls=%async_computation.12 | async-start | bytes 4718592 | tf_op jit(solution)/shard_map/reduce_scatter | solution.py:310
  893.4 455.3 %reduce-scatter.40.cloned.1.call-start = ((), (), s32[]{:S(2)}) async-start(), calls=%async_computation.13 | async-start | bytes 4718592 | tf_op jit(solution)/shard_map/reduce_scatter | solution.py:311
  894.1 558.6 %reduce-scatter.36.cloned.1.call-start = ((), (), s32[]{:S(2)}) async-start(), calls=%async_computation.11 | async-start | bytes 17301504 | tf_op jit(solution)/shard_map/reduce_scatter | solution.py:308
  (185 other events, 1598.8 us)
Sparse Core Ops, SparseCore 0:
  18.5 46.1 all-gather.5
  66.3 26.1 all-gather.7
  94.2 32.3 all-gather.9
  128.0 27.5 all-gather.11
  163.0 33.0 all-gather.13
  218.7 29.2 reduce-scatter.41
  250.4 25.8 reduce-scatter.55
  278.6 21.9 reduce-scatter.51
  302.9 22.5 reduce-scatter.53
  327.6 26.4 reduce-scatter.43
  356.4 25.7 reduce-scatter.45
  384.4 25.7 reduce-scatter.47
  412.6 25.7 reduce-scatter.49
  456.6 44.3 all-gather.5
  502.4 26.1 all-gather.7
  530.0 32.2 all-gather.9
  563.8 27.7 all-gather.11
  599.0 33.0 all-gather.13
  654.4 29.3 reduce-scatter.41
  686.1 25.7 reduce-scatter.55
  714.2 21.9 reduce-scatter.51
  738.5 22.5 reduce-scatter.53
  763.4 26.3 reduce-scatter.43
  792.0 25.8 reduce-scatter.45
  820.2 25.7 reduce-scatter.47
  848.2 25.7 reduce-scatter.49
  897.2 51.9 reduce-scatter.37
  953.5 52.2 reduce-scatter.39
  1008.7 443.9 reduce-scatter.35
Sparse Core Ops, SparseCore 1:
  899.3 449.3 all-reduce.2
